TPU v7x, 32 devices: a whole 2x2x4 slice. The times are simulated.
32 devices in a mesh: row: 4 (over z), col: 8 (over y, x, core).
Axes of the slice: x: 2, y: 2, z: 4, core: 2. Of those that a mesh axis runs over, the one named last changes fastest.
Arguments:
- frontal: float32 [4096, 16384], P('row', 'col'), may hold values from -6 to 6
- sketch: float32 [16384, 256], P('col'), may hold values from -0.046875 to 0.046875
- rank_table: int32 [3, 4], replicated, may hold values from 64 to 256, as said below
Outputs:
- leaf_basis: float32 [4096, 256], P(('row', 'col'))
- top_basis: float32 [4096, 256], P(('row', 'col'))
- coupling: float32 [1024, 16384], P('row', 'col')
Inputs may be any that keep to these rules, and one draw needn't show every extreme that they name: rank_table[l, g] is the rank of the level-l node made of the 2**l consecutive row groups holding g, equal over the groups of that node; a node's rank is at most the larger of its two children's ranks; in every draw some leaf has rank 256 and some leaf rank 256 // 4.
All inputs are finite; a program needn't handle non-finite values.
Results may differ from a plain program's by a relative error of at most 0.00012.
Values sent between devices are 32-bit elements; how exact they have to be, the bound alone decides.
No kernel may reach another device: no remote copies, remote signals or barrier semaphores. Data moves between devices by JAX's collectives and lax.ppermute only.
A program may use at most 64 MiB of HBM per device.

v0:
```python
import jax
import jax.numpy as jnp
from jax import lax
from jax.sharding import PartitionSpec as P

LEVELS = 2


def swapped(block, axis, bit):
    count = lax.axis_size(axis)
    route = []
    for low in range(count):
        high = low | 1 << bit
        if high != low and high < count:
            route += [(low, high), (high, low)]
    return lax.ppermute(block, axis, route)


def product(left, right):
    return jnp.dot(left, right, precision=lax.Precision.HIGHEST, preferred_element_type=jnp.float32)


def mask_of(rank_value, width):
    return (jnp.arange(width) < rank_value).astype(jnp.float32)


def factor(gram_full, keep_mask):
    masked = keep_mask[:, None] * gram_full * keep_mask[None, :] + jnp.diag(1.0 - keep_mask)
    return jnp.linalg.cholesky(masked)


def right_solve(factor_low, operand):
    return lax.linalg.triangular_solve(
        factor_low, operand, left_side=False, lower=True, transpose_a=True
    )


def left_solve(factor_low, operand):
    return lax.linalg.triangular_solve(factor_low, operand, left_side=True, lower=True)


def body(frontal, sketch, rank_table):
    width = sketch.shape[1]
    col_count = lax.axis_size("col")
    share_rows = frontal.shape[0] // col_count
    row_group = lax.axis_index("row")
    column = lax.axis_index("col")
    keep_mask = mask_of(rank_table[0, row_group], width)
    samples = lax.psum(product(frontal, sketch), "col")
    gram_full = product(samples.T, samples)
    factor_low = factor(gram_full, keep_mask)
    full_basis = right_solve(factor_low, samples * keep_mask[None, :])
    coupling = product(full_basis.T, frontal)
    leaf_share = lax.dynamic_slice_in_dim(full_basis, column * share_rows, share_rows, 0)
    coords = left_solve(factor_low, keep_mask[:, None] * gram_full)
    chain_coef = jnp.eye(width, dtype=jnp.float32)
    for height in range(1, LEVELS + 1):
        own_gram = product(coords.T, coords)
        sibling = swapped(own_gram, "row", height - 1)
        pair_gram = own_gram + sibling
        node_mask = mask_of(rank_table[height, row_group], width)
        node_factor = factor(pair_gram, node_mask)
        chain_coef = product(chain_coef, right_solve(node_factor, coords * node_mask[None, :]))
        coords = left_solve(node_factor, node_mask[:, None] * pair_gram)
    top_share = product(leaf_share, chain_coef)
    return (leaf_share, top_share, coupling)


def solution(mesh):
    return jax.shard_map(
        body,
        mesh=mesh,
        in_specs=(P("row", "col"), P("col", None), P()),
        out_specs=(P(("row", "col"), None), P(("row", "col"), None), P("row", "col")),
        check_vma=False,
    )
```

profile of v0, /device:TPU:0, one launch (start us, length us, event | category | flops | bytes accessed | tf_op | source)
XLA Modules:
  0.0 332.8 jit_solution(14702008492156410330)
XLA Ops:
  7.2 1.5 copy-done
  8.8 10.0 %fusion.57 = f32[1024,256]{1,0:T(8,128)} fusion(f32[1024,2048]{1,0:T(8,128)} %param.8, f32[2048,256]{1,0:T(8,128)S(1)} %copy-done), kind=kOutput, calls=%fused_computation.129 | convolution fusion | flops 6442450944 | bytes 11534336 | tf_op jit(solution)/shard_map/dot_general | solution.py:20
  18.8 0.7 constant_dynamic-slice_fusion.4
  22.5 1.3 broadcast_subtract_fusion.1
  23.8 0.7 compare_convert_fusion.1
  24.5 53.9 %all-reduce.3.cloned.1.call-done = f32[1024,256]{1,0:T(8,128)} async-done(((f32[1024,256]{1,0:T(8,128)}), f32[1024,256]{1,0:T(8,128)}) %all-reduce.3.cloned.1.call-update) | async-done | bytes 1048592 | tf_op jit(solution)/shard_map/psum | solution.py:49
  78.4 4.1 %select_add_fusion.2 = (f32[256,256]{0,1:T(8,128)S(1)}, f32[256,256]{0,1:T(8,128)}) fusion(f32[256]{0:T(256)S(1)} %broadcast_subtract_fusion.2, f32[256]{0:T(256)S(1)} %compare_convert_fusion.2, f32[1024,256]{1,0:T(8,128)} %all-reduce.3.cloned.1.call-done), kind=kOutput, calls=%fused_computation.44 | convolution fusion | flops 805634048 | bytes 1574912 | tf_op jit(solution)/shard_map/dot_general | solution.py:20
  82.5 0.9 copy.7
  83.4 1.0 fusion.13
  84.4 0.7 copy-done.4
  85.1 11.7 %cholesky.172 = f32[128,128]{1,0:T(8,128)S(1)} custom-call(f32[128,128]{1,0:T(8,128)S(1)} %cholesky.270), custom_call_target="Cholesky" | custom-call | tf_op jit(solution)/shard_map/jit(cholesky)/cholesky | solution.py:29
  97.0 9.8 %custom-call.22 = f32[1,128,128]{1,2,0:T(8,128)S(1)} custom-call(f32[1,128,128]{2,1,0:T(8,128)S(1)} %get-tuple-element.98), custom_call_target="InvertDiagBlocksLowerTriangular" | custom-call | tf_op jit(solution)/shard_map/jit(cholesky)/cholesky | solution.py:29
  106.8 1.0 fusion.36
  107.8 1.1 convolution_subtract_fusion.6
  109.0 11.9 %cholesky.189 = f32[128,128]{1,0:T(8,128)S(1)} custom-call(f32[128,128]{1,0:T(8,128)S(1)} %convolution_subtract_fusion.6), custom_call_target="Cholesky" | custom-call | tf_op jit(solution)/shard_map/jit(cholesky)/cholesky | solution.py:29
  121.1 0.7 compare_reduce_fusion.4
  123.2 1.3 triangular_solve.69
  125.2 6.8 %while.9 = (s32[]{:T(128)}, f32[256,256]{0,1:T(8,128)S(1)}, s32[2,2]{1,0:T(2,128)}, f32[2,128,128]{2,1,0:T(8,128)}, s32[]{:T(128)}) while((s32[]{:T(128)}, f32[256,256]{0,1:T(8,128)S(1)}, s32[2,2]{1,0:T(2,128)}, f32[2,128,128]{2,1,0:T(8,128)}, s32[]{:T(128)}) %tuple.79), condition=%wide.while_cond.2, body=%wide.while_body.2.sunk | while | flops 2 | bytes 393329 | solution.py:33
  125.2 0.7 constant_dynamic-slice_fusion.9
  126.5 1.3 dynamic-slice.25
  128.6 0.7 constant_dynamic-slice_fusion.9
  129.9 1.3 dynamic-slice.25
  132.0 21.1 %custom-call.17 = f32[2,128,128]{1,2,0:T(8,128)} custom-call(f32[2,128,128]{2,1,0:T(8,128)} %get-tuple-element.29), custom_call_target="InvertDiagBlocksLowerTriangular" | custom-call | tf_op jit(solution)/shard_map/triangular_solve | solution.py:33
  153.1 1.3 fusion.28
  154.4 2.0 convolution_subtract_fusion.3
  156.3 0.7 copy.13
  157.1 1.2 fusion.41
  158.3 2.2 fusion.18
  160.4 1.4 collective-permute-start
  162.0 1.5 fusion.1
  163.4 1.0 convolution_subtract_fusion
  164.4 1.5 fusion.42
  165.9 0.8 copy.23
  166.7 10.9 %fusion = f32[256,2048]{1,0:T(8,128)} fusion(f32[1024,2048]{1,0:T(8,128)} %param.8, f32[1024,128]{0,1:T(8,128)S(1)} %fusion.42, f32[1024,128]{0,1:T(8,128)S(1)} %fusion.1), kind=kOutput, calls=%fused_computation.17 | convolution fusion | flops 6442713088 | bytes 11534336 | tf_op jit(solution)/shard_map/dot_general | solution.py:20
  177.7 1.2 select_add_fusion.1
  179.0 0.7 copy-done.5
  179.7 11.7 %cholesky.206 = f32[128,128]{1,0:T(8,128)S(1)} custom-call(f32[128,128]{1,0:T(8,128)S(1)} %cholesky.273), custom_call_target="Cholesky" | custom-call | tf_op jit(solution)/shard_map/jit(cholesky)/cholesky | solution.py:29
  192.1 9.8 %custom-call.24 = f32[1,128,128]{1,2,0:T(8,128)S(1)} custom-call(f32[1,128,128]{2,1,0:T(8,128)S(1)} %get-tuple-element.96), custom_call_target="InvertDiagBlocksLowerTriangular" | custom-call | tf_op jit(solution)/shard_map/jit(cholesky)/cholesky | solution.py:29
  201.9 1.0 constant_dynamic-update-slice_fusion.2
  203.0 1.1 convolution_subtract_fusion.5
  204.1 11.7 %cholesky.223 = f32[128,128]{1,0:T(8,128)S(1)} custom-call(f32[128,128]{1,0:T(8,128)S(1)} %convolution_subtract_fusion.5), custom_call_target="Cholesky" | custom-call | tf_op jit(solution)/shard_map/jit(cholesky)/cholesky | solution.py:29
  215.9 0.7 compare_reduce_fusion.2
  217.9 5.4 %while.10 = (s32[]{:T(128)}, f32[256,256]{1,0:T(8,128)S(1)}, s32[2,2]{1,0:T(2,128)}, f32[2,128,128]{2,1,0:T(8,128)S(1)}, s32[]{:T(128)}) while((s32[]{:T(128)}, f32[256,256]{1,0:T(8,128)S(1)}, s32[2,2]{1,0:T(2,128)}, f32[2,128,128]{2,1,0:T(8,128)S(1)}, s32[]{:T(128)}) %tuple.82), condition=%wide.while_cond.1, body=%wide.while_body.1.sunk | while | flops 2 | bytes 131189 | solution.py:33
  218.0 0.7 constant_dynamic-slice_fusion.10
  219.2 1.4 bitcast_dynamic-update-slice_fusion.7
  220.7 0.7 constant_dynamic-slice_fusion.10
  221.9 1.4 bitcast_dynamic-update-slice_fusion.7
  223.3 19.8 %custom-call.25 = f32[2,128,128]{1,2,0:T(8,128)S(1)} custom-call(f32[2,128,128]{2,1,0:T(8,128)S(1)} %get-tuple-element.43), custom_call_target="InvertDiagBlocksLowerTriangular" | custom-call | tf_op jit(solution)/shard_map/triangular_solve/custom-call.5 | solution.py:33
  245.3 2.5 collective-permute-start.1
  248.4 10.4 %collective-permute-done.1 = f32[256,256]{0,1:T(8,128)S(1)} collective-permute-done((f32[256,256]{0,1:T(8,128)S(1)}, f32[256,256]{0,1:T(8,128)S(1)}, u32[]{:S(2)}, u32[]{:S(2)}) %collective-permute-start.1) | collective-permute-done | bytes 262176 | tf_op jit(solution)/shard_map/ppermute | solution.py:16
  259.2 0.7 copy-done.6
  259.8 11.7 %cholesky.240 = f32[128,128]{1,0:T(8,128)S(1)} custom-call(f32[128,128]{1,0:T(8,128)S(1)} %cholesky.276), custom_call_target="Cholesky" | custom-call | tf_op jit(solution)/shard_map/jit(cholesky)/cholesky | solution.py:29
  272.2 9.8 %custom-call.27 = f32[1,128,128]{1,2,0:T(8,128)S(1)} custom-call(f32[1,128,128]{2,1,0:T(8,128)S(1)} %get-tuple-element.92), custom_call_target="InvertDiagBlocksLowerTriangular" | custom-call | tf_op jit(solution)/shard_map/jit(cholesky)/cholesky | solution.py:29
  282.1 1.0 constant_dynamic-update-slice_fusion.3
  283.1 1.1 convolution_subtract_fusion.4
  284.2 11.9 %cholesky.257 = f32[128,128]{1,0:T(8,128)S(1)} custom-call(f32[128,128]{1,0:T(8,128)S(1)} %convolution_subtract_fusion.4), custom_call_target="Cholesky" | custom-call | tf_op jit(solution)/shard_map/jit(cholesky)/cholesky | solution.py:29
  296.2 0.7 compare_reduce_fusion
  298.3 5.4 %while.11 = (s32[]{:T(128)}, f32[256,256]{1,0:T(8,128)S(1)}, s32[2,2]{1,0:T(2,128)}, f32[2,128,128]{2,1,0:T(8,128)S(1)}, s32[]{:T(128)}) while((s32[]{:T(128)}, f32[256,256]{1,0:T(8,128)S(1)}, s32[2,2]{1,0:T(2,128)}, f32[2,128,128]{2,1,0:T(8,128)S(1)}, s32[]{:T(128)}) %tuple.85), condition=%wide.while_cond.1.clone, body=%wide.while_body.1.clone.sunk | while | flops 2 | bytes 131189 | solution.py:33
  298.3 0.7 constant_dynamic-slice_fusion.11
  299.5 1.4 bitcast_dynamic-update-slice_fusion.8
  301.0 0.7 constant_dynamic-slice_fusion.11
  302.2 1.4 bitcast_dynamic-update-slice_fusion.8
  303.7 19.7 %custom-call.28 = f32[2,128,128]{1,2,0:T(8,128)S(1)} custom-call(f32[2,128,128]{2,1,0:T(8,128)S(1)} %get-tuple-element.45), custom_call_target="InvertDiagBlocksLowerTriangular" | custom-call | tf_op jit(solution)/shard_map/triangular_solve/custom-call.5 | solution.py:33
  324.7 1.1 fusion.58
  (77 shorter events, 15.4 us)
Async XLA Ops:
  7.2 1.6 copy-start
  7.2 11.6 %copy-start.7 = (s32[3,4]{1,0:T(4,128)S(1)}, s32[3,4]{1,0:T(4,128)}, u32[]{:S(2)}) copy-start(s32[3,4]{1,0:T(4,128)} %param.10) | copy-start | bytes 148
  7.2 71.2 %all-reduce.3.cloned.1.call-start = ((), (), s32[]{:S(2)}) async-start(), calls=%async_computation | async-start | bytes 2097152 | tf_op jit(solution)/shard_map/psum | solution.py:49
  78.4 83.5 %copy-start.1 = (f32[1024,256]{1,0:T(8,128)S(1)}, f32[1024,256]{1,0:T(8,128)}, u32[]{:S(2)}) copy-start(f32[1024,256]{1,0:T(8,128)} %all-reduce.3.cloned.1.call-done) | copy-start | bytes 3145732
  84.4 0.7 copy-start.4
  158.3 6.1 %copy-start.2 = (f32[128,256]{0,1:T(8,128)}, f32[128,256]{0,1:T(8,128)S(1)}, u32[]{:S(2)}) copy-start(f32[128,256]{0,1:T(8,128)S(1)} %fusion.41) | copy-start | bytes 393220
  160.4 17.2 %collective-permute-start = (f32[256,256]{0,1:T(8,128)}, f32[256,256]{0,1:T(8,128)}, u32[]{:S(2)}, u32[]{:S(2)}) collective-permute-start(f32[256,256]{0,1:T(8,128)} %fusion.18), channel_id=1, source_target_pairs={{0,8},{8,0},{16,24},{24,16},{1,9},{9,1},{17,25},{25,17},{2,10},{10... | collective-permute-start | bytes 786440 | tf_op jit(solution)/shard_map/ppermute | solution.py:16
  161.9 15.7 %copy-start.8 = (f32[256]{0:T(256)S(1)}, f32[256]{0:T(256)}, u32[]{:S(2)}) copy-start(f32[256]{0:T(256)} %broadcast_subtract_fusion.1) | copy-start | bytes 3076
  165.9 11.8 %copy-start.3 = (f32[128,256]{0,1:T(8,128)S(1)}, f32[128,256]{0,1:T(8,128)}, u32[]{:S(2)}) copy-start(f32[128,256]{0,1:T(8,128)} %copy-done.2) | copy-start | bytes 393220
  179.0 0.7 copy-start.5
  245.3 13.5 %collective-permute-start.1 = (f32[256,256]{0,1:T(8,128)S(1)}, f32[256,256]{0,1:T(8,128)S(1)}, u32[]{:S(2)}, u32[]{:S(2)}) collective-permute-start(f32[256,256]{0,1:T(8,128)S(1)} %fusion.16), channel_id=1, source_target_pairs={{0,16},{16,0},{8,24},{24,8},{1,17},{17,1},{9,25},{25,9},{2,18},{18... | collective-permute-start | bytes 786440 | tf_op jit(solution)/shard_map/ppermute | solution.py:16
  259.1 0.7 copy-start.6
Sparse Core Ops, SparseCore 0:
  18.9 59.4 all-reduce.2
where the time goes:
time: 337 us; the launch traced here: 333 us
  other arithmetic  172 us (51%)
  waiting for transfers between devices  64.3 us (19%)
  matrix products  47 us (14%)
  local copies, waits for them, and re-layouts  26.8 us (8%)
  between operations  18.8 us (6%)
  starting transfers between devices  3.94 us (1%)
    another operation x20, other arithmetic, factor(): return jnp.linalg.cholesky(masked)  104 us
    another operation x8, other arithmetic, right_solve(): lax.linalg.triangular_solve(factor_low, operand, left_side=False, lower=T...  61.3 us
    psum x1, waiting for transfers between devices, body(): samples = lax.psum(product(frontal, sketch), 'col')  53.9 us
    dot_general x8, matrix products, product(): jnp.dot(left, right, precision=lax.Precision.HIGHEST, preferred_element_t...  29.4 us
    another operation x13, local copies, waits for them, and re-layouts, right_solve(): lax.linalg.triangular_solve(factor_low, operand, left_side=False, lower=T...  12 us
    ppermute x2, waiting for transfers between devices, swapped(): return lax.ppermute(block, axis, route)  10.4 us
    another operation x10, local copies, waits for them, and re-layouts  6.8 us
  transfers between devices with their start and end apart: 3, of which 2 were waited for; matrix products, arithmetic and copies ran while one was open for 7% of the time, Pallas kernels for 0%

commit v1 on v0

--- a/solution.py
+++ b/solution.py
@@ -2,6 +2,7 @@
 import jax.numpy as jnp
 from jax import lax
 from jax.sharding import PartitionSpec as P
+from jax.lax import all_gather
 
 LEVELS = 2
 
@@ -46,7 +47,8 @@
     row_group = lax.axis_index("row")
     column = lax.axis_index("col")
     keep_mask = mask_of(rank_table[0, row_group], width)
-    samples = lax.psum(product(frontal, sketch), "col")
+    vector = product(frontal, sketch)
+    samples = jnp.sum(all_gather(vector, "col"), axis=0)
     gram_full = product(samples.T, samples)
     factor_low = factor(gram_full, keep_mask)
     full_basis = right_solve(factor_low, samples * keep_mask[None, :])

time: 337 us -> 325 us (0.964)
  local copies, waits for them, and re-layouts: 26.8 us -> 19.4 us
  matrix products: 47 us -> 42.2 us
    psum x1 -> x0, waiting for transfers between devices: 53.9 us -> none  [body(): samples = lax.psum(product(frontal, sketch), 'col')]
    all_gather x0 -> x1, waiting for transfers between devices: none -> 52.3 us  [body(): samples = jnp.sum(all_gather(vector, 'col'), axis=0)]
    reduce_sum x0 -> x1, other arithmetic: none -> 4.06 us  [body(): samples = jnp.sum(all_gather(vector, 'col'), axis=0)]
    dot_general x8, matrix products: 29.4 us -> 26.1 us  [product(): jnp.dot(left, right, precision=lax.Precision.HIGHEST, preferred_element_t...]
  transfers between devices with their start and end apart: 3 -> 3, of which waited for: 2 -> 2; matrix products, arithmetic and copies ran while one was open for 7% -> 5% of each run, Pallas kernels for 0% -> 0%
where the time goes in v1:
time: 325 us; the launch traced here: 321 us
  other arithmetic  173 us (53%)
  waiting for transfers between devices  64 us (20%)
  matrix products  42.2 us (13%)
  local copies, waits for them, and re-layouts  19.4 us (6%)
  between operations  18.8 us (6%)
  starting transfers between devices  4.06 us (1%)
    another operation x20, other arithmetic, factor(): return jnp.linalg.cholesky(masked)  104 us
    another operation x8, other arithmetic, right_solve(): lax.linalg.triangular_solve(factor_low, operand, left_side=False, lower=T...  59.8 us
    all_gather x1, waiting for transfers between devices, body(): samples = jnp.sum(all_gather(vector, 'col'), axis=0)  52.3 us
    dot_general x8, matrix products, product(): jnp.dot(left, right, precision=lax.Precision.HIGHEST, preferred_element_t...  26.1 us
    ppermute x2, waiting for transfers between devices, swapped(): return lax.ppermute(block, axis, route)  11.6 us
    another operation x13, local copies, waits for them, and re-layouts, right_solve(): lax.linalg.triangular_solve(factor_low, operand, left_side=False, lower=T...  10.1 us
  transfers between devices with their start and end apart: 3, of which 2 were waited for; matrix products, arithmetic and copies ran while one was open for 5% of the time, Pallas kernels for 0%

profile of v1, /device:TPU:0, one launch (start us, length us, event | category | flops | bytes accessed | tf_op | source)
XLA Modules:
  0.0 321.3 jit_solution(6011935369781617394)
XLA Ops:
  7.2 1.5 copy-done
  8.8 10.0 %fusion.57 = f32[1024,256]{1,0:T(8,128)} fusion(f32[1024,2048]{1,0:T(8,128)} %param.8, f32[2048,256]{1,0:T(8,128)S(1)} %copy-done), kind=kOutput, calls=%fused_computation.129 | convolution fusion | flops 6442450944 | bytes 11534336 | tf_op jit(solution)/shard_map/dot_general | solution.py:21
  18.8 0.6 constant_dynamic-slice_fusion.4
  19.9 0.6 compare_convert_fusion.2
  20.6 0.6 broadcast_subtract_fusion.2
  22.3 0.7 broadcast_subtract_fusion
  23.0 0.7 compare_convert_fusion
  23.6 52.3 %all-gather.3.cloned.1.call-done = f32[8192,256]{1,0:T(8,128)} async-done(((f32[1024,256]{1,0:T(8,128)}), f32[8192,256]{1,0:T(8,128)}) %all-gather.3.cloned.1.call-update) | async-done | bytes 8388624 | tf_op jit(solution)/shard_map/all_gather | solution.py:51
  75.9 4.1 %reduce_sum.9 = f32[1024,256]{1,0:T(8,128)S(1)} reduce(f32[8,1024,256]{2,1,0:T(8,128)} %bitcast.122, f32[]{:T(128)} %constant.84.clone.1), dimensions={0}, to_apply=%region_0.0 | reduce | flops 1835008 | bytes 9437188 | tf_op jit(solution)/shard_map/reduce_sum | solution.py:51
  80.0 1.0 broadcast_multiply_fusion
  81.0 2.5 select_add_fusion.2
  83.7 11.7 %cholesky.172 = f32[128,128]{1,0:T(8,128)S(1)} custom-call(f32[128,128]{1,0:T(8,128)S(1)} %cholesky.270), custom_call_target="Cholesky" | custom-call | tf_op jit(solution)/shard_map/jit(cholesky)/cholesky | solution.py:30
  95.6 9.8 %custom-call.22 = f32[1,128,128]{1,2,0:T(8,128)S(1)} custom-call(f32[1,128,128]{2,1,0:T(8,128)S(1)} %get-tuple-element.98), custom_call_target="InvertDiagBlocksLowerTriangular" | custom-call | tf_op jit(solution)/shard_map/jit(cholesky)/cholesky | solution.py:30
  106.0 11.9 %cholesky.189 = f32[128,128]{1,0:T(8,128)S(1)} custom-call(f32[128,128]{1,0:T(8,128)S(1)} %convolution_subtract_fusion.6), custom_call_target="Cholesky" | custom-call | tf_op jit(solution)/shard_map/jit(cholesky)/cholesky | solution.py:30
  118.1 0.7 compare_reduce_fusion.4
  120.1 0.7 triangular_solve.69
  120.8 4.2 %while.9 = (s32[]{:T(128)}, f32[256,256]{0,1:T(8,128)S(1)}, s32[2,2]{1,0:T(2,128)S(1)}, f32[2,128,128]{2,1,0:T(8,128)S(1)}, s32[]{:T(128)}) while((s32[]{:T(128)}, f32[256,256]{0,1:T(8,128)S(1)}, s32[2,2]{1,0:T(2,128)S(1)}, f32[2,128,128]{2,1,0:T(8,128)S(1)}, s32[]{:T(128)}) %tuple.79), condition=%wide.while_cond.2, body=%wide.while_body.2.sunk | while | flops 2 | bytes 393329 | solution.py:34
  120.8 0.6 fusion.85
  121.4 1.4 dynamic-slice.25
  122.9 0.6 fusion.85
  123.5 1.4 dynamic-slice.25
  125.0 19.7 %custom-call.17 = f32[2,128,128]{1,2,0:T(8,128)S(1)} custom-call(f32[2,128,128]{2,1,0:T(8,128)S(1)} %get-tuple-element.29), custom_call_target="InvertDiagBlocksLowerTriangular" | custom-call | tf_op jit(solution)/shard_map/triangular_solve | solution.py:34
  144.7 1.2 fusion.28
  145.9 2.0 convolution_subtract_fusion.3
  148.0 1.7 fusion.1
  149.6 2.0 convolution_subtract_fusion
  151.7 0.6 fusion.42
  152.4 0.8 copy.23
  153.1 1.2 fusion.41
  154.7 1.6 collective-permute-start
  156.3 10.9 %fusion = f32[256,2048]{1,0:T(8,128)} fusion(f32[1024,2048]{1,0:T(8,128)} %param.8, f32[1024,128]{0,1:T(8,128)S(1)} %fusion.42, f32[1024,128]{0,1:T(8,128)S(1)} %fusion.1), kind=kOutput, calls=%fused_computation.17 | convolution fusion | flops 6442713088 | bytes 11534336 | tf_op jit(solution)/shard_map/dot_general | solution.py:21
  167.5 0.7 copy-done.1
  168.2 11.7 %cholesky.206 = f32[128,128]{1,0:T(8,128)S(1)} custom-call(f32[128,128]{1,0:T(8,128)S(1)} %cholesky.273), custom_call_target="Cholesky" | custom-call | tf_op jit(solution)/shard_map/jit(cholesky)/cholesky | solution.py:30
  180.0 9.8 %custom-call.24 = f32[1,128,128]{1,2,0:T(8,128)S(1)} custom-call(f32[1,128,128]{2,1,0:T(8,128)S(1)} %get-tuple-element.96), custom_call_target="InvertDiagBlocksLowerTriangular" | custom-call | tf_op jit(solution)/shard_map/jit(cholesky)/cholesky | solution.py:30
  189.8 1.0 constant_dynamic-update-slice_fusion.2
  190.8 1.1 convolution_subtract_fusion.5
  191.9 11.7 %cholesky.223 = f32[128,128]{1,0:T(8,128)S(1)} custom-call(f32[128,128]{1,0:T(8,128)S(1)} %convolution_subtract_fusion.5), custom_call_target="Cholesky" | custom-call | tf_op jit(solution)/shard_map/jit(cholesky)/cholesky | solution.py:30
  203.7 0.6 compare_reduce_fusion.3
  204.3 0.7 compare_reduce_fusion.2
  206.4 4.1 %while.10 = (s32[]{:T(128)}, f32[256,256]{1,0:T(8,128)S(1)}, s32[2,2]{1,0:T(2,128)S(1)}, f32[2,128,128]{2,1,0:T(8,128)S(1)}, s32[]{:T(128)}) while((s32[]{:T(128)}, f32[256,256]{1,0:T(8,128)S(1)}, s32[2,2]{1,0:T(2,128)S(1)}, f32[2,128,128]{2,1,0:T(8,128)S(1)}, s32[]{:T(128)}) %tuple.90), condition=%wide.while_cond.1, body=%wide.while_body.1.sunk | while | flops 2 | bytes 131189 | solution.py:34
  206.5 0.6 fusion.86
  207.1 1.4 bitcast_dynamic-update-slice_fusion.7
  208.5 0.6 fusion.86
  209.1 1.4 bitcast_dynamic-update-slice_fusion.7
  210.6 19.8 %custom-call.25 = f32[2,128,128]{1,2,0:T(8,128)S(1)} custom-call(f32[2,128,128]{2,1,0:T(8,128)S(1)} %get-tuple-element.43), custom_call_target="InvertDiagBlocksLowerTriangular" | custom-call | tf_op jit(solution)/shard_map/triangular_solve/custom-call.5 | solution.py:34
  232.5 2.5 collective-permute-start.1
  235.6 11.6 %collective-permute-done.1 = f32[256,256]{0,1:T(8,128)S(1)} collective-permute-done((f32[256,256]{0,1:T(8,128)S(1)}, f32[256,256]{0,1:T(8,128)S(1)}, u32[]{:S(2)}, u32[]{:S(2)}) %collective-permute-start.1) | collective-permute-done | bytes 262176 | tf_op jit(solution)/shard_map/ppermute | solution.py:17
  247.6 0.7 copy-done.2
  248.2 11.7 %cholesky.240 = f32[128,128]{1,0:T(8,128)S(1)} custom-call(f32[128,128]{1,0:T(8,128)S(1)} %cholesky.276), custom_call_target="Cholesky" | custom-call | tf_op jit(solution)/shard_map/jit(cholesky)/cholesky | solution.py:30
  260.0 9.8 %custom-call.27 = f32[1,128,128]{1,2,0:T(8,128)S(1)} custom-call(f32[1,128,128]{2,1,0:T(8,128)S(1)} %get-tuple-element.92), custom_call_target="InvertDiagBlocksLowerTriangular" | custom-call | tf_op jit(solution)/shard_map/jit(cholesky)/cholesky | solution.py:30
  269.8 1.0 constant_dynamic-update-slice_fusion.3
  270.9 1.1 convolution_subtract_fusion.4
  272.0 11.9 %cholesky.257 = f32[128,128]{1,0:T(8,128)S(1)} custom-call(f32[128,128]{1,0:T(8,128)S(1)} %convolution_subtract_fusion.4), custom_call_target="Cholesky" | custom-call | tf_op jit(solution)/shard_map/jit(cholesky)/cholesky | solution.py:30
  283.9 0.6 compare_reduce_fusion.1
  284.6 0.7 compare_reduce_fusion
  286.7 5.4 %while.11 = (s32[]{:T(128)}, f32[256,256]{1,0:T(8,128)S(1)}, s32[2,2]{1,0:T(2,128)}, f32[2,128,128]{2,1,0:T(8,128)S(1)}, s32[]{:T(128)}) while((s32[]{:T(128)}, f32[256,256]{1,0:T(8,128)S(1)}, s32[2,2]{1,0:T(2,128)}, f32[2,128,128]{2,1,0:T(8,128)S(1)}, s32[]{:T(128)}) %tuple.91), condition=%wide.while_cond.1.clone, body=%wide.while_body.1.clone.sunk | while | flops 2 | bytes 131189 | solution.py:34
  286.7 0.7 constant_dynamic-slice_fusion.11
  287.4 0.6 fusion.87
  288.0 1.4 bitcast_dynamic-update-slice_fusion.8
  289.4 0.7 constant_dynamic-slice_fusion.11
  290.1 0.6 fusion.87
  290.7 1.4 bitcast_dynamic-update-slice_fusion.8
  292.1 19.7 %custom-call.28 = f32[2,128,128]{1,2,0:T(8,128)S(1)} custom-call(f32[2,128,128]{2,1,0:T(8,128)S(1)} %get-tuple-element.45), custom_call_target="InvertDiagBlocksLowerTriangular" | custom-call | tf_op jit(solution)/shard_map/triangular_solve/custom-call.5 | solution.py:34
  313.1 1.1 fusion.58
  (72 shorter events, 8.3 us)
Async XLA Ops:
  7.2 1.6 copy-start
  7.2 11.6 %copy-start.3 = (s32[3,4]{1,0:T(4,128)S(1)}, s32[3,4]{1,0:T(4,128)}, u32[]{:S(2)}) copy-start(s32[3,4]{1,0:T(4,128)} %param.10) | copy-start | bytes 148
  7.2 68.8 %all-gather.3.cloned.1.call-start = ((), (), s32[]{:S(2)}) async-start(), calls=%async_computation | async-start | bytes 9437184 | tf_op jit(solution)/shard_map/all_gather | solution.py:51
  125.0 24.6 %copy-start.4 = (s32[2,2]{1,0:T(2,128)}, s32[2,2]{1,0:T(2,128)S(1)}, u32[]{:S(2)}) copy-start(s32[2,2]{1,0:T(2,128)S(1)} %get-tuple-element.256) | copy-start | bytes 52
  154.3 52.2 %copy-start.5 = (s32[2,2]{1,0:T(2,128)S(1)}, s32[2,2]{1,0:T(2,128)}, u32[]{:S(2)}) copy-start(s32[2,2]{1,0:T(2,128)} %copy-done.4) | copy-start | bytes 52
  154.7 12.5 %collective-permute-start = (f32[256,256]{0,1:T(8,128)S(1)}, f32[256,256]{0,1:T(8,128)S(1)}, u32[]{:S(2)}, u32[]{:S(2)}) collective-permute-start(f32[256,256]{0,1:T(8,128)S(1)} %fusion.18), channel_id=1, source_target_pairs={{0,8},{8,0},{16,24},{24,16},{1,9},{9,1},{17,25},{25,17},{2,10},{10... | collective-permute-start | bytes 786440 | tf_op jit(solution)/shard_map/ppermute | solution.py:17
  167.5 0.7 copy-start.1
  232.5 14.7 %collective-permute-start.1 = (f32[256,256]{0,1:T(8,128)S(1)}, f32[256,256]{0,1:T(8,128)S(1)}, u32[]{:S(2)}, u32[]{:S(2)}) collective-permute-start(f32[256,256]{0,1:T(8,128)S(1)} %fusion.16), channel_id=1, source_target_pairs={{0,16},{16,0},{8,24},{24,8},{1,17},{17,1},{9,25},{25,9},{2,18},{18... | collective-permute-start | bytes 786440 | tf_op jit(solution)/shard_map/ppermute | solution.py:17
  247.5 0.7 copy-start.2
Sparse Core Ops, SparseCore 0:
  18.9 56.9 all-gather.2
